TPU v7x, 128 devices: a whole 4x4x4 slice. The times are simulated.
128 devices in a mesh: rows: 64 (over y, x, z), feat: 2 (over core).
Axes of the slice: x: 4, y: 4, z: 4, core: 2. Of those that a mesh axis runs over, the one named last changes fastest.
Arguments:
- blocks: bfloat16 [8192, 8, 128, 128], P('rows', 'feat'), may hold values from -0.1875 to 0.1875
- col_index: int32 [8192, 8], P('rows', 'feat'), may hold values from 0 to 8191, as said below
- row_counts: int32 [8192, 2], P('rows', 'feat'), may hold values from 1 to 4, as said below
- labels: int32 [8192, 128], P('rows'), may hold values 0 or 1
- row_weight: float32 [8192, 128], P('rows'), may hold values from 0.3 to 9
- feature_scale: float32 [8192, 128], P('feat'), may hold values from 0.3 to 3
Outputs:
- solution: float32 [8192, 128], P('feat')
- last_resid: float32 [8192, 128], P('rows')
Inputs may be any that keep to these rules, and one draw needn't show every extreme that they name: `col_index`: a block in slot j of a row block names a feature block of half j // 4, that is from (j // 4) * 4096 to (j // 4 + 1) * 4096 - 1. `row_counts`: some row block of every index of rows has 4 stored blocks in each half; slots from the count on are ignored.
All inputs are finite; a program needn't handle non-finite values. No bound on the sum of `labels` on one device may be relied on, other than what follows from the above.
Results may differ from a plain program's by a relative error of at most 0.0063.
Values may be sent and summed in bfloat16 or wider, within the bound.
No kernel may reach another device: no remote copies, remote signals or barrier semaphores. Data moves between devices by JAX's collectives and lax.ppermute only.
A program may use at most 64 MiB of HBM per device.

v0:
```python
import jax
import jax.numpy as jnp
from jax import lax
from jax.sharding import PartitionSpec as P

ITERS = 2


def body(blocks, col_index, row_counts, labels, row_weight, feature_scale):
    block_side = blocks.shape[2]
    feat_local = feature_scale.shape[0]
    local_col = col_index - lax.axis_index("feat") * feat_local
    live = (lax.broadcasted_iota(jnp.int32, col_index.shape, 1) < row_counts).astype(jnp.float32)

    def backward(resid):
        rowed = (row_weight * resid).astype(jnp.bfloat16)
        terms = jnp.einsum("rsij,ri->rsj", blocks, rowed, preferred_element_type=jnp.float32)
        terms = terms * live[:, :, None]
        partial_value = jax.ops.segment_sum(
            terms.reshape(-1, block_side), local_col.reshape(-1), num_segments=feat_local
        )
        local_sq = jnp.sum(resid * resid)
        squares = lax.psum(local_sq, "rows")
        total = lax.psum(partial_value, "rows")
        return (total, squares)

    def feat_norm(step_vec):
        local_sq = jnp.sum(step_vec * step_vec)
        squares = lax.psum(local_sq, "feat")
        return jnp.sqrt(squares + 1e-06)

    resid = row_weight * (2 * labels - 1).astype(jnp.float32)
    total, squares = backward(resid)
    beta_now = jnp.sqrt(squares + 1e-06)
    unit_rows = resid / beta_now
    step_vec = feature_scale * total / beta_now
    alpha_now = feat_norm(step_vec)
    unit_feat = step_vec / alpha_now
    phi_bar = beta_now
    rho_bar = alpha_now
    search = unit_feat
    solution = jnp.zeros_like(unit_feat)
    for turn in range(ITERS):
        scaled = (feature_scale * unit_feat).astype(jnp.bfloat16)
        picked = jnp.take(scaled, local_col, axis=0)
        forward_terms = jnp.einsum(
            "rsij,rsj->rsi", blocks, picked, preferred_element_type=jnp.float32
        )
        forward_partial_value = jnp.sum(forward_terms * live[:, :, None], axis=1)
        resid = row_weight * lax.psum(forward_partial_value, "feat") - alpha_now * unit_rows
        total, squares = backward(resid)
        beta_now = jnp.sqrt(squares + 1e-06)
        unit_rows = resid / beta_now
        step_vec = feature_scale * total / beta_now - beta_now * unit_feat
        alpha_now = feat_norm(step_vec)
        unit_feat = step_vec / alpha_now
        rho_now = jnp.sqrt(rho_bar * rho_bar + beta_now * beta_now)
        cosine = rho_bar / rho_now
        sine_part = beta_now / rho_now
        theta_now = sine_part * alpha_now
        rho_bar = -cosine * alpha_now
        phi_now = cosine * phi_bar
        phi_bar = sine_part * phi_bar
        solution = solution + phi_now / rho_now * search
        search = unit_feat - theta_now / rho_now * search
    return (solution, resid)


def solution(mesh):
    return jax.shard_map(
        body,
        mesh=mesh,
        in_specs=(
            P("rows", "feat", None, None),
            P("rows", "feat"),
            P("rows", "feat"),
            P("rows", None),
            P("rows", None),
            P("feat", None),
        ),
        out_specs=(P("feat", None), P("rows", None)),
        check_vma=False,
    )
```

profile of v0, /device:TPU:0, one launch (start us, length us, event | category | flops | bytes accessed | tf_op | source)
XLA Modules:
  0.0 674.8 jit_solution(14838331523554784863)
XLA Ops:
  7.2 0.0 all-reduce.5.cloned.1.call-start
  7.2 0.7 fusion.12
  8.0 0.7 compare_and_fusion
  8.7 0.1 copy.10
  8.8 0.1 reshape.56
  8.9 1.5 fusion.13
  10.4 8.0 %fusion.10 = f32[128,1,4,128]{3,1,2,0:T(1,128)S(1)} fusion(bf16[128,4,128,128]{3,2,1,0:T(8,128)(2,1)} %param.8, bf16[128,128,1,1]{1,0,2,3:T(8,128)(2,1)S(1)} %get-tuple-element.13), kind=kOutput, calls=%fused_computation.27 | convolution fusion | flops 16777216 | bytes 17072128 | tf_op jit(solution)/shard_map/rsij,ri->rsj/dot_general | solution.py:17
  18.4 0.2 broadcast_multiply_fusion.1
  18.6 3.6 scatter_custom_fusion
  22.3 0.0 all-reduce.5.cloned.1.call-update
  22.3 0.0 all-reduce.7.cloned.1.call-start
  22.4 181.5 %psum.64 = f32[]{:T(128)} all-reduce(f32[]{:T(128)} %get-tuple-element.14), channel_id=1, replica_groups=mesh['rows'=64,'feat'=2] {'rows'}, use_global_device_ids=true, to_apply=%region_3.0 | all-reduce | flops 1 | bytes 8 | tf_op jit(solution)/shard_map/psum | solution.py:23
  204.5 0.1 copy.12
  204.7 0.1 reshape.76
  204.8 0.1 copy.11
  204.9 0.0 all-reduce.5.cloned.1.call-done
  204.9 4.0 multiply_reduce_fusion.1
  208.9 3.1 psum.65
  212.7 1.8 multiply_convert_fusion.1
  214.6 1.3 gather_fusion
  215.9 0.2 select_bitcast_fusion.1
  216.1 0.0 copy-start.3
  216.1 12.3 %fusion.6 = f32[128,4,1,128]{3,2,1,0:T(1,128)S(1)} fusion(bf16[128,4,128,128]{3,2,1,0:T(8,128)(2,1)} %param.8, bf16[128,4,128,1]{2,1,0,3:T(4,128)(2,1)S(1)} %select_bitcast_fusion.1), kind=kOutput, calls=%fused_computation.17 | convolution fusion | flops 16777216 | bytes 17170432 | tf_op jit(solution)/shard_map/rsij,rsj->rsi/dot_general | solution.py:46
  228.4 0.9 multiply_reduce_fusion.3
  229.3 0.0 all-reduce.7.cloned.1.call-update
  229.3 0.2 all-reduce.9.cloned.1.call-start
  229.5 16.6 %all-reduce.7.cloned.1.call-done = f32[128,128]{1,0:T(8,128)} async-done(((f32[128,128]{1,0:T(8,128)}), f32[128,128]{1,0:T(8,128)}) %all-reduce.7.cloned.1.call-update) | async-done | bytes 65552 | tf_op jit(solution)/shard_map/psum | solution.py:50
  246.1 0.9 fusion.14
  247.0 8.0 %fusion.8 = f32[128,1,4,128]{3,1,2,0:T(1,128)S(1)} fusion(bf16[128,4,128,128]{3,2,1,0:T(8,128)(2,1)} %param.8, bf16[128,128,1,1]{1,0,2,3:T(8,128)(2,1)S(1)} %get-tuple-element.7), kind=kOutput, calls=%fused_computation.25 | convolution fusion | flops 16777216 | bytes 17072128 | tf_op jit(solution)/shard_map/rsij,ri->rsj/dot_general | solution.py:17
  255.1 0.2 broadcast_multiply_fusion
  255.3 3.7 scatter_custom_fusion.1
  259.0 0.0 all-reduce.9.cloned.1.call-update
  259.0 0.0 all-reduce.11.cloned.1.call-start
  259.0 0.6 multiply_reduce_fusion.5
  259.6 180.1 %psum.67 = f32[]{:T(128)} all-reduce(f32[]{:T(128)} %multiply_reduce_fusion.5), channel_id=1, replica_groups=mesh['rows'=64,'feat'=2] {'rows'}, use_global_device_ids=true, to_apply=%region_9.11 | all-reduce | flops 1 | bytes 8 | tf_op jit(solution)/shard_map/psum | solution.py:23
  440.4 0.0 all-reduce.9.cloned.1.call-done
  440.4 4.7 multiply_reduce_fusion
  445.1 3.1 psum.69
  448.9 1.8 multiply_convert_fusion
  450.7 1.3 gather_fusion.1
  452.0 0.2 select_bitcast_fusion
  452.3 12.4 %fusion.4 = f32[128,4,1,128]{3,2,1,0:T(1,128)S(1)} fusion(bf16[128,4,128,128]{3,2,1,0:T(8,128)(2,1)} %param.8, bf16[128,4,128,1]{2,1,0,3:T(4,128)(2,1)S(1)} %select_bitcast_fusion), kind=kOutput, calls=%fused_computation.15 | convolution fusion | flops 16777216 | bytes 17170432 | tf_op jit(solution)/shard_map/rsij,rsj->rsi/dot_general | solution.py:46
  464.6 0.9 multiply_reduce_fusion.2
  465.5 0.0 all-reduce.11.cloned.1.call-update
  465.8 16.6 %all-reduce.11.cloned.1.call-done = f32[128,128]{1,0:T(8,128)} async-done(((f32[128,128]{1,0:T(8,128)}), f32[128,128]{1,0:T(8,128)}) %all-reduce.11.cloned.1.call-update) | async-done | bytes 65552 | tf_op jit(solution)/shard_map/psum | solution.py:50
  482.4 2.1 multiply_reduce_fusion.4
  484.5 179.6 %psum.71 = f32[]{:T(128)} all-reduce(f32[]{:T(128)} %get-tuple-element.3), channel_id=1, replica_groups=mesh['rows'=64,'feat'=2] {'rows'}, use_global_device_ids=true, to_apply=%region_17.19 | all-reduce | flops 1 | bytes 8 | tf_op jit(solution)/shard_map/psum | solution.py:23
  664.9 3.4 multiply_add_fusion
  (9 shorter events, 0.0 us)
Async XLA Ops:
  7.2 197.8 %all-reduce.5.cloned.1.call-start = ((), (), s32[]{:S(2)}) async-start(), calls=%async_computation | async-start | bytes 4194304 | tf_op jit(solution)/shard_map/psum | solution.py:24
  18.6 186.3 %copy-start = (f32[4096,128]{1,0:T(8,128)S(1)}, f32[4096,128]{1,0:T(8,128)}, u32[]{:S(2)}) copy-start(f32[4096,128]{1,0:T(8,128)} %param.13) | copy-start | bytes 6291460
  22.3 223.8 %all-reduce.7.cloned.1.call-start = ((), (), s32[]{:S(2)}) async-start(), calls=%async_computation.1 | async-start | bytes 131072 | tf_op jit(solution)/shard_map/psum | solution.py:50
  216.1 30.0 %copy-start.2 = (f32[128,128]{1,0:T(8,128)S(1)}, f32[128,128]{1,0:T(8,128)}, u32[]{:S(2)}) copy-start(f32[128,128]{1,0:T(8,128)} %param.12) | copy-start | bytes 196612
  216.1 30.0 %copy-start.3 = (s32[128,128]{1,0:T(8,128)S(1)}, s32[128,128]{1,0:T(8,128)}, u32[]{:S(2)}) copy-start(s32[128,128]{1,0:T(8,128)} %param.11) | copy-start | bytes 196612
  229.3 211.1 %all-reduce.9.cloned.1.call-start = ((), (), s32[]{:S(2)}) async-start(), calls=%async_computation.2 | async-start | bytes 4194304 | tf_op jit(solution)/shard_map/psum | solution.py:24
  259.0 223.4 %all-reduce.11.cloned.1.call-start = ((), (), s32[]{:S(2)}) async-start(), calls=%async_computation.3 | async-start | bytes 131072 | tf_op jit(solution)/shard_map/psum | solution.py:50
  452.3 212.6 %copy-start.1 = (f32[4096,128]{1,0:T(8,128)S(1)}, f32[4096,128]{1,0:T(8,128)}, u32[]{:S(2)}) copy-start(f32[4096,128]{1,0:T(8,128)} %get-tuple-element.12) | copy-start | bytes 6291460
Sparse Core Ops, SparseCore 0:
  22.4 135.0 all-reduce.4
  229.4 16.6 all-reduce.6
  259.1 133.9 all-reduce.8
  465.7 16.6 all-reduce.10
where the time goes:
time: 675 us
  blocking collectives  547 us (81%)
  matrix products  40.7 us (6%)
  waiting for transfers between devices  33.3 us (5%)
  other arithmetic  32.2 us (5%)
  between operations  17.7 us (3%)
    psum x3, blocking collectives, backward(): squares = lax.psum(local_sq, 'rows')  541 us
    psum x2, waiting for transfers between devices, body(): lax.psum(forward_partial_value, 'feat')  33.2 us
    dot_general x2, matrix products, body(): jnp.einsum('rsij,rsj->rsi', blocks, picked, preferred_element_type=jnp.fl...  24.6 us
    dot_general x2, matrix products, backward(): jnp.einsum('rsij,ri->rsj', blocks, rowed, preferred_element_type=jnp.floa...  16.1 us
  transfers between devices with their start and end apart: 4, of which 2 were waited for; matrix products, arithmetic and copies ran while one was open for 0% of the time, Pallas kernels for 0%

commit v1 on v0

--- a/solution.py
+++ b/solution.py
@@ -4,6 +4,11 @@
 from jax.sharding import PartitionSpec as P
 
 ITERS = 2
+
+
+def watch_the_scales(z_in, ax_name):
+    state_now = jnp.sum(lax.all_gather(z_in, ax_name), 0)
+    return state_now
 
 
 def body(blocks, col_index, row_counts, labels, row_weight, feature_scale):
@@ -47,7 +52,7 @@
             "rsij,rsj->rsi", blocks, picked, preferred_element_type=jnp.float32
         )
         forward_partial_value = jnp.sum(forward_terms * live[:, :, None], axis=1)
-        resid = row_weight * lax.psum(forward_partial_value, "feat") - alpha_now * unit_rows
+        resid = row_weight * watch_the_scales(forward_partial_value, "feat") - alpha_now * unit_rows
         total, squares = backward(resid)
         beta_now = jnp.sqrt(squares + 1e-06)
         unit_rows = resid / beta_now

time: 675 us -> 630 us (0.933)
  waiting for transfers between devices: 33.3 us -> 0.08 us
  blocking collectives: 547 us -> 538 us
    psum x2 -> x0, waiting for transfers between devices: 33.2 us -> none  [body(): lax.psum(forward_partial_value, 'feat')]
    psum x3, blocking collectives: 541 us -> 528 us  [backward(): squares = lax.psum(local_sq, 'rows')]
  transfers between devices with their start and end apart: 4 -> 2, of which waited for: 2 -> 0; matrix products, arithmetic and copies ran while one was open for 0% -> 0% of each run, Pallas kernels for 0% -> 0%
where the time goes in v1:
time: 630 us
  blocking collectives  538 us (85%)
  matrix products  40.7 us (6%)
  other arithmetic  29.2 us (5%)
  between operations  18 us (3%)
    psum x3, blocking collectives, backward(): squares = lax.psum(local_sq, 'rows')  528 us
    dot_general x2, matrix products, body(): jnp.einsum('rsij,rsj->rsi', blocks, picked, preferred_element_type=jnp.fl...  24.7 us
    dot_general x2, matrix products, backward(): jnp.einsum('rsij,ri->rsj', blocks, rowed, preferred_element_type=jnp.floa...  16.1 us
  transfers between devices with their start and end apart: 2, of which 0 were waited for; matrix products, arithmetic and copies ran while one was open for 0% of the time, Pallas kernels for 0%

profile of v1, /device:TPU:0, one launch (start us, length us, event | category | flops | bytes accessed | tf_op | source)
XLA Modules:
  0.0 629.8 jit_solution(15332653727602939242)
XLA Ops:
  7.2 0.0 all-reduce.3.cloned.1.call-start
  7.2 0.7 fusion.12
  8.0 0.7 compare_and_fusion
  8.7 0.1 copy.15
  8.8 0.1 reshape.56
  8.9 1.5 fusion.13
  10.4 8.0 %fusion.10 = f32[128,1,4,128]{3,1,2,0:T(1,128)S(1)} fusion(bf16[128,4,128,128]{3,2,1,0:T(8,128)(2,1)} %param.8, bf16[128,128,1,1]{1,0,2,3:T(8,128)(2,1)S(1)} %get-tuple-element.13), kind=kOutput, calls=%fused_computation.27 | convolution fusion | flops 16777216 | bytes 17072128 | tf_op jit(solution)/shard_map/rsij,ri->rsj/dot_general | solution.py:22
  18.4 0.2 broadcast_multiply_fusion.1
  18.6 0.0 copy-start
  18.6 3.6 scatter_custom_fusion
  22.3 0.0 all-reduce.3.cloned.1.call-update
  22.3 0.0 all-reduce.5.cloned.1.call-start
  22.4 181.5 %psum.50 = f32[]{:T(128)} all-reduce(f32[]{:T(128)} %get-tuple-element.14), channel_id=1, replica_groups=mesh['rows'=64,'feat'=2] {'rows'}, use_global_device_ids=true, to_apply=%region_3.0 | all-reduce | flops 1 | bytes 8 | tf_op jit(solution)/shard_map/psum | solution.py:28
  204.5 0.1 copy.17
  204.7 0.1 reshape.78
  204.8 0.1 copy.16
  204.9 0.0 all-reduce.3.cloned.1.call-done
  204.9 0.0 copy-done
  204.9 4.0 multiply_reduce_fusion.1
  208.9 3.1 psum.51
  212.7 1.8 multiply_convert_fusion.1
  214.6 1.3 gather_fusion
  215.9 0.2 select_bitcast_fusion.1
  216.1 0.0 copy-start.2
  216.1 0.0 copy-start.3
  216.1 12.3 %fusion.6 = f32[128,4,1,128]{3,2,1,0:T(1,128)S(1)} fusion(bf16[128,4,128,128]{3,2,1,0:T(8,128)(2,1)} %param.8, bf16[128,4,128,1]{2,1,0,3:T(4,128)(2,1)S(1)} %select_bitcast_fusion.1), kind=kOutput, calls=%fused_computation.17 | convolution fusion | flops 16777216 | bytes 17170432 | tf_op jit(solution)/shard_map/rsij,rsj->rsi/dot_general | solution.py:51
  228.4 0.2 multiply_reduce_fusion.3
  228.7 2.1 all-gather
  230.8 8.0 %fusion.8 = f32[128,1,4,128]{3,1,2,0:T(1,128)S(1)} fusion(bf16[128,4,128,128]{3,2,1,0:T(8,128)(2,1)} %param.8, bf16[128,128,1,1]{1,0,2,3:T(8,128)(2,1)S(1)} %get-tuple-element.7), kind=kOutput, calls=%fused_computation.25 | convolution fusion | flops 16777216 | bytes 17072128 | tf_op jit(solution)/shard_map/rsij,ri->rsj/dot_general | solution.py:22
  238.9 0.2 broadcast_multiply_fusion
  239.1 3.7 scatter_custom_fusion.1
  242.8 0.0 all-reduce.5.cloned.1.call-update
  242.8 0.6 multiply_reduce_fusion.5
  243.4 172.8 %psum.52 = f32[]{:T(128)} all-reduce(f32[]{:T(128)} %multiply_reduce_fusion.5), channel_id=1, replica_groups=mesh['rows'=64,'feat'=2] {'rows'}, use_global_device_ids=true, to_apply=%region_9.11 | all-reduce | flops 1 | bytes 8 | tf_op jit(solution)/shard_map/psum | solution.py:28
  417.0 0.0 all-reduce.5.cloned.1.call-done
  417.1 4.7 multiply_reduce_fusion
  421.7 3.1 psum.54
  425.5 1.8 multiply_convert_fusion
  427.3 1.3 gather_fusion.1
  428.7 0.2 select_bitcast_fusion
  428.9 0.0 copy-start.1
  428.9 12.4 %fusion.4 = f32[128,4,1,128]{3,2,1,0:T(1,128)S(1)} fusion(bf16[128,4,128,128]{3,2,1,0:T(8,128)(2,1)} %param.8, bf16[128,4,128,1]{2,1,0,3:T(4,128)(2,1)S(1)} %select_bitcast_fusion), kind=kOutput, calls=%fused_computation.15 | convolution fusion | flops 16777216 | bytes 17170432 | tf_op jit(solution)/shard_map/rsij,rsj->rsi/dot_general | solution.py:51
  441.3 0.3 multiply_reduce_fusion.2
  441.5 1.9 all-gather.1
  443.4 1.3 multiply_reduce_fusion.4
  444.7 174.0 %psum.55 = f32[]{:T(128)} all-reduce(f32[]{:T(128)} %get-tuple-element.3), channel_id=1, replica_groups=mesh['rows'=64,'feat'=2] {'rows'}, use_global_device_ids=true, to_apply=%region_17.19 | all-reduce | flops 1 | bytes 8 | tf_op jit(solution)/shard_map/psum | solution.py:28
  619.6 0.0 copy-done.1
  619.6 3.4 multiply_add_fusion
  (7 shorter events, 0.1 us)
Async XLA Ops:
  7.2 197.8 %all-reduce.3.cloned.1.call-start = ((), (), s32[]{:S(2)}) async-start(), calls=%async_computation | async-start | bytes 4194304 | tf_op jit(solution)/shard_map/psum | solution.py:29
  18.6 186.3 %copy-start = (f32[4096,128]{1,0:T(8,128)S(1)}, f32[4096,128]{1,0:T(8,128)}, u32[]{:S(2)}) copy-start(f32[4096,128]{1,0:T(8,128)} %param.13) | copy-start | bytes 6291460
  22.3 394.7 %all-reduce.5.cloned.1.call-start = ((), (), s32[]{:S(2)}) async-start(), calls=%async_computation.1 | async-start | bytes 4194304 | tf_op jit(solution)/shard_map/psum | solution.py:29
  216.1 14.6 %copy-start.2 = (f32[128,128]{1,0:T(8,128)S(1)}, f32[128,128]{1,0:T(8,128)}, u32[]{:S(2)}) copy-start(f32[128,128]{1,0:T(8,128)} %param.12) | copy-start | bytes 196612
  216.1 14.6 %copy-start.3 = (s32[128,128]{1,0:T(8,128)S(1)}, s32[128,128]{1,0:T(8,128)}, u32[]{:S(2)}) copy-start(s32[128,128]{1,0:T(8,128)} %param.11) | copy-start | bytes 196612
  428.9 190.7 %copy-start.1 = (f32[4096,128]{1,0:T(8,128)S(1)}, f32[4096,128]{1,0:T(8,128)}, u32[]{:S(2)}) copy-start(f32[4096,128]{1,0:T(8,128)} %get-tuple-element.12) | copy-start | bytes 6291460
Sparse Core Ops, SparseCore 0:
  22.4 135.0 all-reduce.2
  242.9 126.0 all-reduce.4
